TPU v7x, 32 devices: a whole 2x2x4 slice. The times are simulated.
32 devices in a mesh: mesh: 8 (over z, y), mode: 4 (over x, core).
Axes of the slice: x: 2, y: 2, z: 4, core: 2. Of those that a mesh axis runs over, the one named last changes fastest.
Arguments:
- field: float32 [256, 131072], P('mode', 'mesh'), may hold values from -6 to 6
- right_side: float32 [256, 131072], P('mode', 'mesh'), may hold values from -6 to 6
- coefficient: float32 [2, 131072], P(None, 'mesh'), may hold values from 0.3 to 3
- precond: float32 [131072], P('mesh'), may hold values from 0.1 to 1
- blocks: bfloat16 [2, 7, 256, 256], replicated, may hold values from -0.125 to 0.125
- couplings: int32 [512, 7], P('mesh'), may hold values from 0 to 1, as said below
- chaos_values: bfloat16 [48, 16, 16], replicated, may hold values from -0.875 to 0.875
- chaos_index: int32 [48, 2], replicated, may hold values from 0 to 15, as said below
Outputs:
- updated: float32 [256, 131072], P('mode', 'mesh')
- residual: float32 [256, 131072], P('mode', 'mesh')
Inputs may be any that keep to these rules, and one draw needn't show every extreme that they name: couplings[i, c] links block i to block i + c - 3; it is 1 for c = 3 and wherever block i + c - 3 lies in another slab of 16384 unknowns. `chaos_index`: rows 3 r to 3 r + 2 hold row block r, with column blocks r and two other distinct blocks.
All inputs are finite; a program needn't handle non-finite values.
Results may differ from a plain program's by a relative error of at most 0.0032.
Values may be sent and summed in bfloat16 or wider, within the bound.
A program may use at most 128 MiB of HBM per device.

v0:
```python
import jax
import jax.numpy as jnp
from jax import lax
from jax.sharding import PartitionSpec as P

P_SIZE = 256
PBLK = 16
B = 256


def padded_2(cells, sides, width):
    for axis, dim in sides:
        count = lax.axis_size(axis)
        ends = count - 1
        head = lax.slice_in_dim(cells, 0, width, axis=dim)
        tail = lax.slice_in_dim(cells, cells.shape[dim] - width, cells.shape[dim], axis=dim)
        cells = jnp.concatenate(
            [
                lax.ppermute(tail, axis, [(i, (i + 1) % count) for i in range(ends)]),
                cells,
                lax.ppermute(head, axis, [((i + 1) % count, i) for i in range(ends)]),
            ],
            axis=dim,
        )
    return cells


def stiffness(padded, local_width, blocks, couplings, coefficient, which_term):
    mode_count = padded.shape[0]
    block_count = local_width // B
    summed = jnp.zeros((mode_count, block_count, B), jnp.float32)
    for offset in range(7):
        window = lax.slice_in_dim(padded, offset * B, offset * B + block_count * B, axis=1)
        window = window.reshape(mode_count, block_count, B)
        product = jnp.einsum(
            "pnb,bd->pnd", window, blocks[which_term, offset], preferred_element_type=jnp.float32
        )
        summed = summed + product * couplings[:, offset].astype(jnp.float32)[None, :, None]
    return summed.reshape(mode_count, -1) * coefficient[which_term][None, :]


def chaos_matrix(chaos_values, chaos_index):
    block_ids = jnp.arange(PBLK, dtype=jnp.int32)
    row_hits = (chaos_index[:, 0:1] == block_ids[None, :]).astype(jnp.float32)
    col_hits = (chaos_index[:, 1:2] == block_ids[None, :]).astype(jnp.float32)
    spread_blocks = jnp.einsum(
        "br,bc,bij->ricj", row_hits, col_hits, chaos_values.astype(jnp.float32)
    )
    return spread_blocks.reshape(P_SIZE, P_SIZE).astype(jnp.bfloat16)


def shards(field, right_side, coefficient, precond, blocks, couplings, chaos_values, chaos_index):
    local_width = field.shape[1]
    mode_count = field.shape[0]
    lowered = field.astype(jnp.bfloat16)
    padded = padded_2(lowered, (("mesh", 1),), 3 * B)
    spread = stiffness(padded, local_width, blocks, couplings, coefficient, 1).astype(jnp.bfloat16)
    diffused = stiffness(padded, local_width, blocks, couplings, coefficient, 0)
    matrix = chaos_matrix(chaos_values, chaos_index)
    my_rows = lax.dynamic_slice_in_dim(matrix, lax.axis_index("mode") * mode_count, mode_count, 0)
    mixed = jnp.dot(
        my_rows,
        lax.all_gather(spread, "mode", axis=0, tiled=True),
        preferred_element_type=jnp.float32,
    )
    residual = right_side - (diffused + mixed)
    updated = field + precond[None, :] * residual
    return (updated, residual)


def solution(mesh):
    placed = (
        P("mode", "mesh"),
        P("mode", "mesh"),
        P(None, "mesh"),
        P("mesh"),
        P(),
        P("mesh", None),
        P(),
        P(),
    )
    return jax.shard_map(
        shards,
        mesh=mesh,
        in_specs=placed,
        out_specs=(P("mode", "mesh"), P("mode", "mesh")),
        check_vma=False,
    )
```

profile of v0, /device:TPU:0, one launch (start us, length us, event | category | flops | bytes accessed | tf_op | source)
XLA Modules:
  0.0 129.4 jit_solution(411362106234384962)
XLA Ops:
  7.2 2.5 %convert_element_type.95 = bf16[64,16384]{1,0:T(8,128)(2,1)S(1)} convert(f32[64,16384]{1,0:T(8,128)} %param.8) | non-fusion elementwise | flops 1048576 | bytes 6291456 | tf_op jit(solution)/shard_map/convert_element_type | solution.py:55
  9.8 4.9 %collective-permute-start = (bf16[64,768]{1,0:T(8,128)(2,1)S(1)}, bf16[64,768]{1,0:T(8,128)(2,1)S(1)}, u32[]{:S(2)}, u32[]{:S(2)}) collective-permute-start(bf16[64,768]{1,0:T(8,128)(2,1)S(1)} %get-tuple-element.11), channel_id=1, source_target_pairs={{0,4},{4,8},{8,12},{12,16},{16,20},{20,24},{24,28},{1,5},{5,9},{9,... | collective-permute-start | bytes 294920 | tf_op jit(solution)/shard_map/ppermute | solution.py:19
  14.7 1.3 collective-permute-start.1
  17.5 3.8 %collective-permute-done.1 = bf16[64,768]{1,0:T(8,128)(2,1)S(1)} collective-permute-done((bf16[64,768]{1,0:T(8,128)(2,1)S(1)}, bf16[64,768]{1,0:T(8,128)(2,1)S(1)}, u32[]{:S(2)}, u32[]{:S(2)}) %collective-permute-start.1) | collective-permute-done | bytes 98336 | tf_op jit(solution)/shard_map/ppermute | solution.py:21
  21.2 5.6 %pad_maximum_fusion = (bf16[64,16384]{1,0:T(8,128)(2,1)S(1)}, bf16[64,16384]{1,0:T(8,128)(2,1)S(1)}, bf16[64,16384]{1,0:T(8,128)(2,1)S(1)}, bf16[64,16384]{1,0:T...) fusion(bf16[64,768]{1,0:T(8,128)(2,1)S(1)} %collective-permute-done.1, ...), kind=kLoop, calls=%fused_computation.14 | loop fusion | flops 25165824 | bytes 14876672 | tf_op jit(solution)/shard_map/concatenate | solution.py:17
  30.2 0.7 fusion.13
  30.9 0.7 fusion.15
  31.6 0.7 fusion.17
  32.3 2.7 %fusion.7 = f32[64,64,256]{2,1,0:T(8,128)} fusion(bf16[64,64,256]{2,1,0:T(8,128)(2,1)S(1)} %bitcast.138, bf16[2,7,256,256]{3,2,1,0:T(8,128)(2,1)S(1)} %copy-done.14), kind=kOutput, calls=%fused_computation.19 | convolution fusion | flops 536870912 | bytes 6422528 | tf_op jit(solution)/shard_map/pnb,bd->pnd/dot_general | solution.py:35
  35.1 2.7 %fusion.9 = f32[64,64,256]{2,1,0:T(8,128)} fusion(bf16[64,64,256]{2,1,0:T(8,128)(2,1)S(1)} %bitcast.140, bf16[2,7,256,256]{3,2,1,0:T(8,128)(2,1)S(1)} %copy-done.14), kind=kOutput, calls=%fused_computation.21 | convolution fusion | flops 536870912 | bytes 6422528 | tf_op jit(solution)/shard_map/pnb,bd->pnd/dot_general | solution.py:35
  37.8 6.5 %multiply_add_fusion.1 = f32[64,64,256]{2,1,0:T(8,128)} fusion(f32[64,64,256]{2,1,0:T(8,128)} %fusion.7, f32[64,64,256]{2,1,0:T(8,128)} %fusion.9, f32[64,64,256]{2,1,0:T(8,128)S(1)} %fusion.11, f32[64,64,256]{2,1,0:T(8,128)S(1)} %fusion.13, f32[64,64,256]{2,1,0:T(8,128)S(1)} %fusion.15, f32[64,64,256]{2,1,0:T(8,128)S(1)} %fusion.17, ...), kind=kOutput, calls=%fused_computation.4 | convolution fusion | flops 550502400 | bytes 31591936 | tf_op jit(solution)/shard_map/pnb,bd->pnd/dot_general | solution.py:35
  44.3 4.6 %copy.20 = f32[8,8,64,256]{3,1,2,0:T(8,128)S(1)} copy(f32[8,8,64,256]{3,2,1,0:T(8,128)} %bitcast.153) | data formatting | bytes 8388608
  48.9 1.7 %multiply_convert_fusion = bf16[64,16384]{1,0:T(8,128)(2,1)} fusion(f32[64,16384]{1,0:T(8,128)S(1)} %bitcast.151, f32[16384]{0:T(1024)S(1)} %bitcast.161), kind=kLoop, calls=%fused_computation.3 | loop fusion | flops 2097152 | bytes 6356992 | tf_op jit(solution)/shard_map/convert_element_type | solution.py:57
  51.7 1.0 convert_element_type.112
  52.7 1.8 %fusion.25 = f32[64,64,256]{2,1,0:T(8,128)S(1)} fusion(bf16[64,64,256]{2,1,0:T(8,128)(2,1)S(1)} %bitcast.137, bf16[2,7,256,256]{3,2,1,0:T(8,128)(2,1)} %param.12), kind=kOutput, calls=%fused_computation.37 | convolution fusion | flops 536870912 | bytes 6422528 | tf_op jit(solution)/shard_map/pnb,bd->pnd/dot_general | solution.py:35
  54.5 1.8 %fusion.21 = f32[64,64,256]{2,1,0:T(8,128)S(1)} fusion(bf16[64,64,256]{2,1,0:T(8,128)(2,1)S(1)} %bitcast.139, bf16[2,7,256,256]{3,2,1,0:T(8,128)(2,1)} %param.12), kind=kOutput, calls=%fused_computation.33 | convolution fusion | flops 536870912 | bytes 6422528 | tf_op jit(solution)/shard_map/pnb,bd->pnd/dot_general | solution.py:35
  56.3 1.8 %fusion.23 = f32[64,64,256]{2,1,0:T(8,128)S(1)} fusion(bf16[64,64,256]{2,1,0:T(8,128)(2,1)S(1)} %bitcast.141, bf16[2,7,256,256]{3,2,1,0:T(8,128)(2,1)} %param.12), kind=kOutput, calls=%fused_computation.35 | convolution fusion | flops 536870912 | bytes 6422528 | tf_op jit(solution)/shard_map/pnb,bd->pnd/dot_general | solution.py:35
  58.1 1.8 %fusion.27 = f32[64,64,256]{2,1,0:T(8,128)S(1)} fusion(bf16[64,64,256]{2,1,0:T(8,128)(2,1)S(1)} %bitcast.143, bf16[2,7,256,256]{3,2,1,0:T(8,128)(2,1)} %param.12), kind=kOutput, calls=%fused_computation.39 | convolution fusion | flops 536870912 | bytes 6422528 | tf_op jit(solution)/shard_map/pnb,bd->pnd/dot_general | solution.py:35
  60.1 1.8 %fusion.29 = f32[64,64,256]{2,1,0:T(8,128)S(1)} fusion(bf16[64,64,256]{2,1,0:T(8,128)(2,1)S(1)} %bitcast.145, bf16[2,7,256,256]{3,2,1,0:T(8,128)(2,1)} %param.12), kind=kOutput, calls=%fused_computation.41 | convolution fusion | flops 536870912 | bytes 6422528 | tf_op jit(solution)/shard_map/pnb,bd->pnd/dot_general | solution.py:35
  62.1 3.8 %fusion.31 = f32[64,64,256]{2,1,0:T(8,128)} fusion(bf16[64,64,256]{2,1,0:T(8,128)(2,1)S(1)} %bitcast.147, bf16[2,7,256,256]{3,2,1,0:T(8,128)(2,1)} %param.12), kind=kOutput, calls=%fused_computation.43 | convolution fusion | flops 536870912 | bytes 6422528 | tf_op jit(solution)/shard_map/pnb,bd->pnd/dot_general | solution.py:35
  65.9 5.3 %multiply_add_fusion.2 = f32[64,64,256]{2,1,0:T(8,128)} fusion(f32[64,64,256]{2,1,0:T(8,128)S(1)} %fusion.21, f32[64,64,256]{2,1,0:T(8,128)S(1)} %fusion.23, f32[64,64,256]{2,1,0:T(8,128)S(1)} %fusion.25, f32[64,64,256]{2,1,0:T(8,128)S(1)} %fusion.27, f32[64,64,256]{2,1,0:T(8,128)S(1)} %fusion.29, f32[64,64,256]{2,1,0:T(8,128)} %fusion.31, ...), kind=kOutput, calls=%fused_computation.5 | convolution fusion | flops 550502400 | bytes 31590144 | tf_op jit(solution)/shard_map/pnb,bd->pnd/dot_general | solution.py:35
  71.2 6.6 %copy.19 = f32[8,8,64,256]{3,1,2,0:T(8,128)} copy(f32[8,8,64,256]{3,2,1,0:T(8,128)} %bitcast.152) | data formatting | bytes 8388608
  77.8 32.3 %all-gather.2.cloned.1.call-done = bf16[256,16384]{1,0:T(8,128)(2,1)} async-done(((bf16[64,16384]{1,0:T(8,128)(2,1)}), bf16[256,16384]{1,0:T(8,128)(2,1)}) %all-gather.2.cloned.1.call-update) | async-done | bytes 8388624 | tf_op jit(solution)/shard_map/all_gather | solution.py:63
  110.1 12.4 %multiply_add_fusion = (f32[64,16384]{1,0:T(8,128)}, f32[64,16384]{1,0:T(8,128)}) fusion(f32[64,16384]{1,0:T(8,128)} %param.8, f32[16384]{0:T(1024)S(1)} %copy-done.16, f32[64,16384]{1,0:T(8,128)} %param.9, bf16[256,16384]{1,0:T(8,128)(2,1)} %all-gather.2.cloned.1.call-done, bf16[256,256]{1,0:T(8,128)(2,1)S(1)} %convert_element_type.112, s32[]{:T(128)S(6)} %select_n.3, ...), kind=kOutput, calls=%fused_computation.2 | convolution fusion | flops 542113792 | bytes 29523972 | tf_op jit(solution)/shard_map/dot_general | solution.py:61
  (56 shorter events, 6.3 us)
Async XLA Ops:
  7.2 43.4 %copy-start = (bf16[48,16,16]{0,2,1:T(8,128)(2,1)S(1)}, bf16[48,16,16]{0,2,1:T(8,128)(2,1)}, u32[]{:S(2)}) copy-start(bf16[48,16,16]{0,2,1:T(8,128)(2,1)} %param.14) | copy-start | bytes 73732
  7.2 9.4 %copy-start.15 = (f32[2,16384]{1,0:T(2,128)S(1)}, f32[2,16384]{1,0:T(2,128)}, u32[]{:S(2)}) copy-start(f32[2,16384]{1,0:T(2,128)} %param.10) | copy-start | bytes 393220
  7.2 102.9 %all-gather.2.cloned.1.call-start = ((), (), s32[]{:S(2)}) async-start(), calls=%async_computation | async-start | bytes 10485760 | tf_op jit(solution)/shard_map/all_gather | solution.py:63
  7.2 9.5 %copy-start.14 = (bf16[2,7,256,256]{3,2,1,0:T(8,128)(2,1)S(1)}, bf16[2,7,256,256]{3,2,1,0:T(8,128)(2,1)}, u32[]{:S(2)}) copy-start(bf16[2,7,256,256]{3,2,1,0:T(8,128)(2,1)} %param.12) | copy-start | bytes 5505028
  9.8 7.6 %collective-permute-start = (bf16[64,768]{1,0:T(8,128)(2,1)S(1)}, bf16[64,768]{1,0:T(8,128)(2,1)S(1)}, u32[]{:S(2)}, u32[]{:S(2)}) collective-permute-start(bf16[64,768]{1,0:T(8,128)(2,1)S(1)} %get-tuple-element.11), channel_id=1, source_target_pairs={{0,4},{4,8},{8,12},{12,16},{16,20},{20,24},{24,28},{1,5},{5,9},{9,... | collective-permute-start | bytes 294920 | tf_op jit(solution)/shard_map/ppermute | solution.py:19
  14.7 6.5 %collective-permute-start.1 = (bf16[64,768]{1,0:T(8,128)(2,1)S(1)}, bf16[64,768]{1,0:T(8,128)(2,1)S(1)}, u32[]{:S(2)}, u32[]{:S(2)}) collective-permute-start(bf16[64,768]{1,0:T(8,128)(2,1)S(1)} %get-tuple-element.12), channel_id=1, source_target_pairs={{4,0},{8,4},{12,8},{16,12},{20,16},{24,20},{28,24},{5,1},{9,5},{13... | collective-permute-start | bytes 294920 | tf_op jit(solution)/shard_map/ppermute | solution.py:21
  16.6 0.8 copy-start.17
  27.4 5.0 %copy-start.2 = (bf16[8,8,64,256]{3,2,1,0:T(8,128)(2,1)}, bf16[8,8,64,256]{3,2,1,0:T(8,128)(2,1)S(1)}, u32[]{:S(2)}) copy-start(bf16[8,8,64,256]{3,2,1,0:T(8,128)(2,1)S(1)} %copy.17) | copy-start | bytes 6291460
  27.9 7.1 %copy-start.4 = (bf16[8,8,64,256]{3,2,1,0:T(8,128)(2,1)}, bf16[8,8,64,256]{3,2,1,0:T(8,128)(2,1)S(1)}, u32[]{:S(2)}) copy-start(bf16[8,8,64,256]{3,2,1,0:T(8,128)(2,1)S(1)} %copy.16) | copy-start | bytes 6291460
  28.5 1.7 %copy-start.6 = (bf16[8,8,64,256]{3,2,1,0:T(8,128)(2,1)}, bf16[8,8,64,256]{3,2,1,0:T(8,128)(2,1)S(1)}, u32[]{:S(2)}) copy-start(bf16[8,8,64,256]{3,2,1,0:T(8,128)(2,1)S(1)} %copy.14) | copy-start | bytes 6291460
  29.1 1.8 %copy-start.8 = (bf16[8,8,64,256]{3,2,1,0:T(8,128)(2,1)}, bf16[8,8,64,256]{3,2,1,0:T(8,128)(2,1)S(1)}, u32[]{:S(2)}) copy-start(bf16[8,8,64,256]{3,2,1,0:T(8,128)(2,1)S(1)} %copy.13) | copy-start | bytes 6291460
  29.6 2.0 %copy-start.10 = (bf16[8,8,64,256]{3,2,1,0:T(8,128)(2,1)}, bf16[8,8,64,256]{3,2,1,0:T(8,128)(2,1)S(1)}, u32[]{:S(2)}) copy-start(bf16[8,8,64,256]{3,2,1,0:T(8,128)(2,1)S(1)} %copy.12) | copy-start | bytes 6291460
  30.2 7.6 %copy-start.12 = (bf16[8,8,64,256]{3,2,1,0:T(8,128)(2,1)}, bf16[8,8,64,256]{3,2,1,0:T(8,128)(2,1)S(1)}, u32[]{:S(2)}) copy-start(bf16[8,8,64,256]{3,2,1,0:T(8,128)(2,1)S(1)} %copy.18) | copy-start | bytes 6291460
  48.8 1.7 %copy-start.18 = (s32[48,2]{0,1:T(2,128)S(1)}, s32[48,2]{0,1:T(2,128)}, u32[]{:S(2)}) copy-start(s32[48,2]{0,1:T(2,128)} %param.15) | copy-start | bytes 1156
  52.7 1.8 %copy-start.3 = (bf16[8,8,64,256]{3,2,1,0:T(8,128)(2,1)S(1)}, bf16[8,8,64,256]{3,2,1,0:T(8,128)(2,1)}, u32[]{:S(2)}) copy-start(bf16[8,8,64,256]{3,2,1,0:T(8,128)(2,1)} %copy-done.2) | copy-start | bytes 6291460
  54.5 1.8 %copy-start.5 = (bf16[8,8,64,256]{3,2,1,0:T(8,128)(2,1)S(1)}, bf16[8,8,64,256]{3,2,1,0:T(8,128)(2,1)}, u32[]{:S(2)}) copy-start(bf16[8,8,64,256]{3,2,1,0:T(8,128)(2,1)} %copy-done.4) | copy-start | bytes 6291460
  56.3 1.8 %copy-start.7 = (bf16[8,8,64,256]{3,2,1,0:T(8,128)(2,1)S(1)}, bf16[8,8,64,256]{3,2,1,0:T(8,128)(2,1)}, u32[]{:S(2)}) copy-start(bf16[8,8,64,256]{3,2,1,0:T(8,128)(2,1)} %copy-done.6) | copy-start | bytes 6291460
  58.1 2.0 %copy-start.9 = (bf16[8,8,64,256]{3,2,1,0:T(8,128)(2,1)S(1)}, bf16[8,8,64,256]{3,2,1,0:T(8,128)(2,1)}, u32[]{:S(2)}) copy-start(bf16[8,8,64,256]{3,2,1,0:T(8,128)(2,1)} %copy-done.8) | copy-start | bytes 6291460
  60.1 2.0 %copy-start.11 = (bf16[8,8,64,256]{3,2,1,0:T(8,128)(2,1)S(1)}, bf16[8,8,64,256]{3,2,1,0:T(8,128)(2,1)}, u32[]{:S(2)}) copy-start(bf16[8,8,64,256]{3,2,1,0:T(8,128)(2,1)} %copy-done.10) | copy-start | bytes 6291460
  62.1 3.8 %copy-start.13 = (bf16[8,8,64,256]{3,2,1,0:T(8,128)(2,1)S(1)}, bf16[8,8,64,256]{3,2,1,0:T(8,128)(2,1)}, u32[]{:S(2)}) copy-start(bf16[8,8,64,256]{3,2,1,0:T(8,128)(2,1)} %copy-done.12) | copy-start | bytes 6291460
  71.2 38.9 %copy-start.16 = (f32[16384]{0:T(1024)S(1)}, f32[16384]{0:T(1024)}, u32[]{:S(2)}) copy-start(f32[16384]{0:T(1024)} %param.11) | copy-start | bytes 196612
  110.1 12.4 %copy-start.1 = (bf16[48,16,16]{0,2,1:T(8,128)(2,1)S(1)}, bf16[48,16,16]{0,2,1:T(8,128)(2,1)}, u32[]{:S(2)}) copy-start(bf16[48,16,16]{0,2,1:T(8,128)(2,1)} %param.14) | copy-start | bytes 73732
Sparse Core Ops, SparseCore 0:
  50.7 59.4 all-gather.1
where the time goes:
time: 130 us; the launch traced here: 129 us
  matrix products  45.6 us (35%)
  waiting for transfers between devices  36.1 us (28%)
  local copies, waits for them, and re-layouts  17.3 us (13%)
  between operations  14.4 us (11%)
  other arithmetic  9.79 us (8%)
  starting transfers between devices  6.23 us (5%)
    dot_general x14, matrix products, stiffness(): jnp.einsum('pnb,bd->pnd', window, blocks[which_term, offset], preferred_e...  32.7 us
    all_gather x1, waiting for transfers between devices, shards(): lax.all_gather(spread, 'mode', axis=0, tiled=True)  32.3 us
    unnamed x47, local copies, waits for them, and re-layouts  15.5 us
    dot_general x1, matrix products, shards(): jnp.dot(my_rows, lax.all_gather(spread, 'mode', axis=0, tiled=True), pref...  12.4 us
    concatenate x1, other arithmetic, padded_2(): jnp.concatenate([lax.ppermute(tail, axis, [(i, (i + 1) % count) for i in...  5.58 us
    ppermute x1, starting transfers between devices, padded_2(): lax.ppermute(tail, axis, [(i, (i + 1) % count) for i in range(ends)])  4.9 us
    ppermute x1, waiting for transfers between devices, padded_2(): lax.ppermute(head, axis, [((i + 1) % count, i) for i in range(ends)])  3.78 us
  transfers between devices with their start and end apart: 3, of which 2 were waited for; matrix products, arithmetic and copies ran while one was open for 22% of the time, Pallas kernels for 0%

commit v1 on v0

v1 whole, which is shorter than its diff:
```python
import functools

import jax
import jax.numpy as jnp
from jax import lax
from jax.experimental import pallas as pl
from jax.experimental.pallas import tpu as pltpu
from jax.sharding import PartitionSpec as P

MESH = pl.DeviceIdType.MESH
REACH = 3


def kernel(
    modes, slabs, group,
    field, right, coefficient, blocks, couplings, chaos_values, chaos_index,
    out,
    low, fbuf, rbuf, weights, coef, gathered, matrix,
    field_sem, right_sem, weight_sem, coef_sem, out_sem,
    halo_send, halo_recv, near_send, far_send, forward_send, recv,
):
    rows, width = field.shape
    size = blocks.shape[-1]
    count = width // size
    groups = count // group
    span = group * size
    taps = 2 * REACH + 1
    pairs = modes // 2
    me = lax.axis_index("mode")
    slab = lax.axis_index("mesh")
    sibling = me + 1 - 2 * lax.rem(me, 2)
    peers = [lax.rem(me + 2 * j, modes) for j in range(1, pairs)]
    has_left = slab > 0
    has_right = slab < slabs - 1

    def columns(g):
        return pl.ds(pl.multiple_of(g * span, span), span)

    def field_copy(g):
        return pltpu.make_async_copy(field.at[:, columns(g)], fbuf.at[:, columns(g)], field_sem.at[g])

    def right_copy(g):
        return pltpu.make_async_copy(right.at[:, columns(g)], rbuf.at[:, columns(g)], right_sem.at[g])

    def weight_copy(k):
        return pltpu.make_async_copy(blocks.at[k], weights.at[k], weight_sem.at[k])

    def out_copy(g):
        return pltpu.make_async_copy(rbuf.at[:, columns(g)], out.at[:, columns(g)], out_sem.at[g])

    field_copy(0).start()
    field_copy(groups - 1).start()
    weight_copy(1).start()
    coef_copy = pltpu.make_async_copy(coefficient, coef, coef_sem)
    coef_copy.start()

    @pl.loop(1, groups - 1)
    def _(g):
        field_copy(g).start()

    weight_copy(0).start()

    @pl.loop(0, groups)
    def _(g):
        right_copy(g).start()

    barrier = pltpu.get_barrier_semaphore()
    for other in [sibling] + peers:
        pl.semaphore_signal(barrier, inc=1, device_id={"mode": other}, device_id_type=MESH)

    @pl.when(has_left)
    def _():
        pl.semaphore_signal(barrier, inc=1, device_id={"mesh": slab - 1}, device_id_type=MESH)

    @pl.when(has_right)
    def _():
        pl.semaphore_signal(barrier, inc=1, device_id={"mesh": slab + 1}, device_id_type=MESH)

    def lower(g):
        for b in range(group):
            at = g * group + b
            cols = pl.ds(pl.multiple_of(at * size, size), size)
            low[REACH + at] = fbuf[:, cols].astype(jnp.bfloat16)

    field_copy(0).wait()
    lower(0)
    field_copy(groups - 1).wait()
    lower(groups - 1)

    pl.semaphore_wait(barrier, pairs + jnp.minimum(slab, 1) + jnp.minimum(slabs - 1 - slab, 1))

    to_left = pltpu.make_async_remote_copy(
        src_ref=low.at[pl.ds(REACH, REACH)], dst_ref=low.at[pl.ds(REACH + count, REACH)],
        send_sem=halo_send.at[0], recv_sem=halo_recv.at[0],
        device_id={"mesh": slab - 1}, device_id_type=MESH)
    to_right = pltpu.make_async_remote_copy(
        src_ref=low.at[pl.ds(count, REACH)], dst_ref=low.at[pl.ds(0, REACH)],
        send_sem=halo_send.at[1], recv_sem=halo_recv.at[1],
        device_id={"mesh": slab + 1}, device_id_type=MESH)

    @pl.when(has_left)
    def _():
        to_left.start()

    @pl.when(has_right)
    def _():
        to_right.start()

    @pl.when(jnp.logical_not(has_left))
    def _():
        low[pl.ds(0, REACH)] = jnp.zeros((REACH, rows, size), jnp.bfloat16)

    @pl.when(jnp.logical_not(has_right))
    def _():
        low[pl.ds(REACH + count, REACH)] = jnp.zeros((REACH, rows, size), jnp.bfloat16)

    field_copy(1).wait()
    lower(1)
    weight_copy(1).wait()
    coef_copy.wait()

    def stencil(g, k):
        tall = []
        for b in range(group):
            at = g * group + b
            wide = []
            for c in range(taps):
                keep = jnp.full((rows, size), couplings[c, at].astype(jnp.float32)).astype(jnp.bfloat16)
                wide.append(low[at + c] * keep)
            tall.append(jnp.concatenate(wide, axis=1))
        stacked = jnp.concatenate(tall, axis=0)
        return jnp.dot(stacked, weights[k].reshape(taps * size, size), preferred_element_type=jnp.float32)

    def piece(slot, g):
        return gathered.at[slot, pl.ds(g * group, group)]

    def send(slot, g, target, sem):
        return pltpu.make_async_remote_copy(
            src_ref=piece(slot, g), dst_ref=piece(slot, g), send_sem=sem, recv_sem=recv.at[slot, g],
            device_id={"mode": target}, device_id_type=MESH)

    def turn(t):
        return lax.rem(t + 1, groups)

    @pl.loop(0, groups)
    def _(t):
        g = turn(t)

        @pl.when(t + 2 <= groups - 2)
        def _():
            field_copy(t + 2).wait()
            lower(t + 2)

        @pl.when(jnp.logical_and(t == groups - 2, has_right))
        def _():
            to_left.wait_recv()

        @pl.when(jnp.logical_and(t == groups - 1, has_left))
        def _():
            to_right.wait_recv()

        sums = stencil(g, 1)
        for b in range(group):
            at = g * group + b
            cols = pl.ds(pl.multiple_of(at * size, size), size)
            scaled = sums[b * rows:(b + 1) * rows] * coef[1:2, cols]
            gathered[me, at] = scaled.astype(jnp.bfloat16)
        for j, peer in enumerate(peers):
            send(me, g, peer, far_send.at[j, g]).start()
        send(me, g, sibling, near_send.at[g]).start()

    part = chaos_values.shape[1]
    parts = modes * rows // part
    lane_of = lax.broadcasted_iota(jnp.int32, (part, modes * rows), 1)
    row_of = lax.broadcasted_iota(jnp.int32, (part, modes * rows), 0)
    repeat = (lax.rem(lane_of, part) == row_of).astype(jnp.float32).astype(jnp.bfloat16)
    block_of = lane_of // part
    links = chaos_values.shape[0] // parts
    for q in range(rows // part):
        total = jnp.zeros((part, modes * rows), jnp.float32)
        for e in range(links):
            at = (me * (rows // part) + q) * links + e
            spread_out = jnp.dot(chaos_values[at], repeat, preferred_element_type=jnp.float32)
            total = total + jnp.where(block_of == chaos_index[1, at], spread_out, 0.0)
        matrix[q * part:(q + 1) * part, :] = total.astype(jnp.bfloat16)

    weight_copy(0).wait()

    @pl.loop(0, groups)
    def _(t):
        g = turn(t)
        right_copy(g).wait()
        sums = stencil(g, 0)
        for b in range(group):
            at = g * group + b
            cols = pl.ds(pl.multiple_of(at * size, size), size)
            rbuf[:, cols] = rbuf[:, cols] - sums[b * rows:(b + 1) * rows] * coef[0:1, cols]

    def mix(g):
        send(sibling, g, sibling, near_send.at[g]).wait_recv()
        for j, peer in enumerate(peers):
            other = peer + 1 - 2 * lax.rem(peer, 2)
            send(other, g, sibling, forward_send.at[j, g]).wait_recv()
        for b in range(group):
            at = g * group + b
            cols = pl.ds(pl.multiple_of(at * size, size), size)
            mixed = jnp.dot(
                matrix[...], gathered[:, at].reshape(modes * rows, size), preferred_element_type=jnp.float32)
            rbuf[:, cols] = rbuf[:, cols] - mixed
        out_copy(g).start()

    def forward(g):
        for j, peer in enumerate(peers):
            send(peer, g, peer, far_send.at[j, g]).wait_recv()
            send(peer, g, sibling, forward_send.at[j, g]).start()

    forward(turn(0))

    @pl.loop(1, groups)
    def _(t):
        forward(turn(t))
        mix(turn(t - 1))

    mix(turn(groups - 1))

    @pl.loop(0, groups)
    def _(g):
        send(me, g, sibling, near_send.at[g]).wait_send()
        for j, peer in enumerate(peers):
            send(me, g, peer, far_send.at[j, g]).wait_send()
            send(peer, g, sibling, forward_send.at[j, g]).wait_send()
        out_copy(g).wait()

    @pl.when(has_left)
    def _():
        to_left.wait_send()

    @pl.when(has_right)
    def _():
        to_right.wait_send()


def finish_kernel(field, found, precond, updated, residual):
    value = found[...]
    residual[...] = value
    updated[...] = field[...] + precond[...] * value


def shards(modes, slabs, field, right_side, coefficient, precond, blocks, couplings, chaos_values, chaos_index):
    rows, width = field.shape
    size = blocks.shape[-1]
    taps = blocks.shape[1]
    count = width // size
    group = 4
    groups = count // group
    others = max(modes // 2 - 1, 1)
    anywhere = pl.BlockSpec(memory_space=pl.ANY)
    scalars = pl.BlockSpec(memory_space=pltpu.SMEM)
    dma = pltpu.SemaphoreType.DMA
    found = pl.pallas_call(
        functools.partial(kernel, modes, slabs, group),
        out_shape=jax.ShapeDtypeStruct((rows, width), jnp.float32),
        in_specs=[anywhere, anywhere, anywhere, anywhere, scalars, pl.BlockSpec(memory_space=pltpu.VMEM), scalars],
        out_specs=anywhere,
        scratch_shapes=[
            pltpu.VMEM((count + 2 * REACH, rows, size), jnp.bfloat16),
            pltpu.VMEM((rows, width), jnp.float32),
            pltpu.VMEM((rows, width), jnp.float32),
            pltpu.VMEM(blocks.shape, jnp.bfloat16),
            pltpu.VMEM(coefficient.shape, jnp.float32),
            pltpu.VMEM((modes, count, rows, size), jnp.bfloat16),
            pltpu.VMEM((rows, modes * rows), jnp.bfloat16),
            dma((groups,)), dma((groups,)), dma((2,)), dma, dma((groups,)),
            dma((2,)), dma((2,)), dma((groups,)), dma((others, groups)), dma((others, groups)),
            dma((modes, groups)),
        ],
        compiler_params=pltpu.CompilerParams(
            collective_id=0, has_side_effects=True, vmem_limit_bytes=56 * 1024 * 1024),
        name="gather_mix",
    )(field, right_side, coefficient, blocks, couplings.T, chaos_values, chaos_index.T)
    step = min(2048, width)
    tile = pl.BlockSpec((rows, step), lambda i: (0, i))
    return pl.pallas_call(
        finish_kernel,
        grid=(width // step,),
        out_shape=[jax.ShapeDtypeStruct((rows, width), jnp.float32)] * 2,
        in_specs=[tile, tile, pl.BlockSpec((1, step), lambda i: (0, i))],
        out_specs=[tile, tile],
        name="finish",
    )(field, found, precond[None, :])


def solution(mesh):
    placed = (
        P("mode", "mesh"),
        P("mode", "mesh"),
        P(None, "mesh"),
        P("mesh"),
        P(),
        P("mesh", None),
        P(),
        P(),
    )
    return jax.shard_map(
        functools.partial(shards, mesh.shape["mode"], mesh.shape["mesh"]),
        mesh=mesh,
        in_specs=placed,
        out_specs=(P("mode", "mesh"), P("mode", "mesh")),
        check_vma=False,
    )
```

time: 130 us -> 66.7 us (0.51)
  Pallas kernels: 0 us -> 63.3 us
  matrix products: 45.6 us -> 0 us
  waiting for transfers between devices: 36.1 us -> 0 us
  local copies, waits for them, and re-layouts: 17.3 us -> 1.71 us
  between operations: 14.4 us -> 0.64 us
  other arithmetic: 9.79 us -> 0 us
  starting transfers between devices: 6.23 us -> 0 us
    pallas_call x0 -> x2, Pallas kernels: none -> 63.3 us  [the longest x1 54.3 us: shards(): pl.pallas_call(functools.partial(kernel, modes, slabs, group), out_shape=...]
    dot_general x16 -> x0, matrix products: 45.6 us -> none  [the longest x14 32.7 us: stiffness(): jnp.einsum('pnb,bd->pnd', window, blocks[which_term, offset], preferred_e...]
    all_gather x1 -> x0, waiting for transfers between devices: 32.3 us -> none  [shards(): lax.all_gather(spread, 'mode', axis=0, tiled=True)]
    unnamed x47 -> x1, local copies, waits for them, and re-layouts: 15.5 us -> 1.71 us
    ppermute x2 -> x0, starting transfers between devices: 6.2 us -> none  [the longest x1 4.9 us: padded_2(): lax.ppermute(tail, axis, [(i, (i + 1) % count) for i in range(ends)])]
    concatenate x1 -> x0, other arithmetic: 5.58 us -> none  [padded_2(): jnp.concatenate([lax.ppermute(tail, axis, [(i, (i + 1) % count) for i in...]
    convert_element_type x3 -> x0, other arithmetic: 4.2 us -> none  [the longest x1 2.53 us: shards(): lowered = field.astype(jnp.bfloat16)]
    ppermute x2 -> x0, waiting for transfers between devices: 3.78 us -> none  [the longest x1 3.78 us: padded_2(): lax.ppermute(head, axis, [((i + 1) % count, i) for i in range(ends)])]
  transfers between devices with their start and end apart: 3 -> 0, of which waited for: 2 -> 0; matrix products, arithmetic and copies ran while one was open for 22% -> 0% of each run, Pallas kernels for 0% -> 0%
where the time goes in v1:
time: 66.7 us; the launch traced here: 65.7 us
  Pallas kernels  63.3 us (95%)
  local copies, waits for them, and re-layouts  1.71 us (3%)
    pallas_call x1, Pallas kernels, shards(): pl.pallas_call(functools.partial(kernel, modes, slabs, group), out_shape=...  54.3 us
    pallas_call x1, Pallas kernels, shards(): pl.pallas_call(finish_kernel, grid=(width // step,), out_shape=[jax.Shape...  9.05 us
    unnamed x1, local copies, waits for them, and re-layouts  1.71 us

profile of v1, /device:TPU:0, one launch (start us, length us, event | category | flops | bytes accessed | tf_op | source)
XLA Modules:
  0.0 65.7 jit_solution(2483582997177921279)
XLA Ops:
  0.6 1.7 %copy.10.chaos_values = bf16[48,16,16]{2,1,0:T(8,128)(2,1)} copy(bf16[48,16,16]{0,2,1:T(8,128)(2,1)} %param.14) | data formatting | bytes 49152 | tf_op args[6]
  2.3 54.3 %gather_mix.1.found = f32[64,16384]{1,0:T(8,128)} custom-call(f32[64,16384]{1,0:T(8,128)} %field.3, f32[64,16384]{1,0:T(8,128)} %right.1, f32[2,16384]{1,0:T(2,128)} %coefficient.1, bf16[2,7,256,256]{3,2,1,0:T(8,128)(2,1)} %blocks.1, s32[7,64]{1,0:T(8,128)} %bitcast.4, bf16[48,16,16]{2,1,0:T(8,128)(2,1)} %copy.10.chaos_values, s32[2,48]{1,0:T(2,128)} %bitcast.5), custom_call_target="tpu_custom_call" | custom-call | tf_op jit(solution)/shard_map/gather_mix/pallas_call | solution.py:260
  56.6 9.0 %finish.1 = (f32[64,16384]{1,0:T(8,128)}, f32[64,16384]{1,0:T(8,128)}) custom-call(f32[64,16384]{1,0:T(8,128)} %field.3, f32[64,16384]{1,0:T(8,128)} %gather_mix.1.found, f32[1,16384]{1,0:T(1,128)} %bitcast.3), custom_call_target="tpu_custom_call" | custom-call | tf_op jit(solution)/shard_map/finish/pallas_call | solution.py:283

commit v2 on v1

--- a/solution.py
+++ b/solution.py
@@ -14,9 +14,9 @@
 def kernel(
     modes, slabs, group,
     field, right, coefficient, blocks, couplings, chaos_values, chaos_index,
-    out,
-    low, fbuf, rbuf, weights, coef, gathered, matrix,
-    field_sem, right_sem, weight_sem, coef_sem, out_sem,
+    fbuf, rbuf,
+    low, weights, coef, gathered, matrix, hits,
+    field_sem, right_sem, weight_sem, coef_sem,
     halo_send, halo_recv, near_send, far_send, forward_send, recv,
 ):
     rows, width = field.shape
@@ -45,9 +45,6 @@
     def weight_copy(k):
         return pltpu.make_async_copy(blocks.at[k], weights.at[k], weight_sem.at[k])
 
-    def out_copy(g):
-        return pltpu.make_async_copy(rbuf.at[:, columns(g)], out.at[:, columns(g)], out_sem.at[g])
-
     field_copy(0).start()
     field_copy(groups - 1).start()
     weight_copy(1).start()
@@ -169,20 +166,26 @@
             send(me, g, peer, far_send.at[j, g]).start()
         send(me, g, sibling, near_send.at[g]).start()
 
-    part = chaos_values.shape[1]
-    parts = modes * rows // part
-    lane_of = lax.broadcasted_iota(jnp.int32, (part, modes * rows), 1)
-    row_of = lax.broadcasted_iota(jnp.int32, (part, modes * rows), 0)
-    repeat = (lax.rem(lane_of, part) == row_of).astype(jnp.float32).astype(jnp.bfloat16)
-    block_of = lane_of // part
-    links = chaos_values.shape[0] // parts
-    for q in range(rows // part):
-        total = jnp.zeros((part, modes * rows), jnp.float32)
-        for e in range(links):
-            at = (me * (rows // part) + q) * links + e
-            spread_out = jnp.dot(chaos_values[at], repeat, preferred_element_type=jnp.float32)
-            total = total + jnp.where(block_of == chaos_index[1, at], spread_out, 0.0)
-        matrix[q * part:(q + 1) * part, :] = total.astype(jnp.bfloat16)
+    part, _, links = chaos_values.shape
+    total_rows = modes * rows
+    per_row = links * part // total_rows
+    column_of = lax.broadcasted_iota(jnp.int32, (1, total_rows), 1) // part
+    for n in range(links):
+        hits[n:n + 1, :] = (column_of == chaos_index[1, n]).astype(jnp.float32)
+    lane_of = lax.broadcasted_iota(jnp.int32, (part, total_rows), 1)
+    step_of = lax.broadcasted_iota(jnp.int32, (part, total_rows), 0)
+    repeat = (lax.rem(lane_of, part) == step_of).astype(jnp.float32).astype(jnp.bfloat16)
+    row_of = lax.broadcasted_iota(jnp.int32, (rows, links), 0)
+    owner_of = lax.broadcasted_iota(jnp.int32, (rows, links), 1) // per_row
+    owned = owner_of == row_of // part + me * (rows // part)
+    built = jnp.zeros((rows, total_rows), jnp.float32)
+    for i in range(part):
+        spread_out = lax.dot_general(
+            chaos_values[i], repeat, (((0,), (0,)), ((), ())), preferred_element_type=jnp.float32)
+        placed = (spread_out * hits[...]).astype(jnp.bfloat16)
+        mine = jnp.logical_and(owned, lax.rem(row_of, part) == i).astype(jnp.float32).astype(jnp.bfloat16)
+        built = built + jnp.dot(mine, placed, preferred_element_type=jnp.float32)
+    matrix[...] = built.astype(jnp.bfloat16)
 
     weight_copy(0).wait()
 
@@ -207,7 +210,6 @@
             mixed = jnp.dot(
                 matrix[...], gathered[:, at].reshape(modes * rows, size), preferred_element_type=jnp.float32)
             rbuf[:, cols] = rbuf[:, cols] - mixed
-        out_copy(g).start()
 
     def forward(g):
         for j, peer in enumerate(peers):
@@ -229,7 +231,6 @@
         for j, peer in enumerate(peers):
             send(me, g, peer, far_send.at[j, g]).wait_send()
             send(peer, g, sibling, forward_send.at[j, g]).wait_send()
-        out_copy(g).wait()
 
     @pl.when(has_left)
     def _():
@@ -240,10 +241,30 @@
         to_right.wait_send()
 
 
-def finish_kernel(field, found, precond, updated, residual):
-    value = found[...]
-    residual[...] = value
-    updated[...] = field[...] + precond[...] * value
+def finish_kernel(pieces, field, found, precond, updated, residual, stage, sems):
+    rows, width = field.shape
+    span = width // pieces
+
+    def columns(i):
+        return pl.ds(pl.multiple_of(i * span, span), span)
+
+    def found_copy(i):
+        return pltpu.make_async_copy(found.at[:, columns(i)], residual.at[:, columns(i)], sems.at[0, i])
+
+    def stage_copy(i):
+        return pltpu.make_async_copy(stage.at[:, columns(i)], updated.at[:, columns(i)], sems.at[1, i])
+
+    @pl.loop(0, pieces)
+    def _(i):
+        found_copy(i).start()
+        cols = columns(i)
+        stage[:, cols] = field[:, cols] + precond[:, cols] * found[:, cols]
+        stage_copy(i).start()
+
+    @pl.loop(0, pieces)
+    def _(i):
+        found_copy(i).wait()
+        stage_copy(i).wait()
 
 
 def shards(modes, slabs, field, right_side, coefficient, precond, blocks, couplings, chaos_values, chaos_index):
@@ -254,40 +275,41 @@
     group = 4
     groups = count // group
     others = max(modes // 2 - 1, 1)
+    inside = pl.BlockSpec(memory_space=pltpu.VMEM)
     anywhere = pl.BlockSpec(memory_space=pl.ANY)
+    spare = 67043328 - 2 * rows * width * 4 - 96 * 1024
     scalars = pl.BlockSpec(memory_space=pltpu.SMEM)
     dma = pltpu.SemaphoreType.DMA
-    found = pl.pallas_call(
+    kept, found = pl.pallas_call(
         functools.partial(kernel, modes, slabs, group),
-        out_shape=jax.ShapeDtypeStruct((rows, width), jnp.float32),
+        out_shape=[pltpu.VMEM((rows, width), jnp.float32)] * 2,
         in_specs=[anywhere, anywhere, anywhere, anywhere, scalars, pl.BlockSpec(memory_space=pltpu.VMEM), scalars],
-        out_specs=anywhere,
+        out_specs=[inside] * 2,
         scratch_shapes=[
             pltpu.VMEM((count + 2 * REACH, rows, size), jnp.bfloat16),
-            pltpu.VMEM((rows, width), jnp.float32),
-            pltpu.VMEM((rows, width), jnp.float32),
             pltpu.VMEM(blocks.shape, jnp.bfloat16),
             pltpu.VMEM(coefficient.shape, jnp.float32),
             pltpu.VMEM((modes, count, rows, size), jnp.bfloat16),
             pltpu.VMEM((rows, modes * rows), jnp.bfloat16),
-            dma((groups,)), dma((groups,)), dma((2,)), dma, dma((groups,)),
+            pltpu.VMEM((chaos_values.shape[0], modes * rows), jnp.float32),
+            dma((groups,)), dma((groups,)), dma((2,)), dma,
             dma((2,)), dma((2,)), dma((groups,)), dma((others, groups)), dma((others, groups)),
             dma((modes, groups)),
         ],
         compiler_params=pltpu.CompilerParams(
-            collective_id=0, has_side_effects=True, vmem_limit_bytes=56 * 1024 * 1024),
+            collective_id=0, has_side_effects=True, vmem_limit_bytes=spare),
         name="gather_mix",
-    )(field, right_side, coefficient, blocks, couplings.T, chaos_values, chaos_index.T)
-    step = min(2048, width)
-    tile = pl.BlockSpec((rows, step), lambda i: (0, i))
+    )(field, right_side, coefficient, blocks, couplings.T, chaos_values.transpose(1, 2, 0), chaos_index.T)
+    pieces = 16
     return pl.pallas_call(
-        finish_kernel,
-        grid=(width // step,),
+        functools.partial(finish_kernel, pieces),
         out_shape=[jax.ShapeDtypeStruct((rows, width), jnp.float32)] * 2,
-        in_specs=[tile, tile, pl.BlockSpec((1, step), lambda i: (0, i))],
-        out_specs=[tile, tile],
+        in_specs=[inside] * 3,
+        out_specs=[anywhere] * 2,
+        scratch_shapes=[pltpu.VMEM((rows, width), jnp.float32), dma((2, pieces))],
+        compiler_params=pltpu.CompilerParams(vmem_limit_bytes=8 * 1024 * 1024),
         name="finish",
-    )(field, found, precond[None, :])
+    )(kept, found, precond[None, :])
 
 
 def solution(mesh):

time: 66.7 us -> 58.4 us (0.88); the launches traced: 65.7 us -> 58.1 us
  Pallas kernels: 63.3 us -> 57.5 us
  local copies, waits for them, and re-layouts: 1.71 us -> 0.01 us
    pallas_call x1, Pallas kernels: 9.05 us -> 3.54 us  [shards(): pl.pallas_call(functools.partial(finish_kernel, pieces), out_shape=[jax.S...]
    unnamed x1 -> x2, local copies, waits for them, and re-layouts: 1.71 us -> 0.01 us
where the time goes in v2:
time: 58.4 us; the launch traced here: 58.1 us
  Pallas kernels  57.5 us (98%)
  between operations  0.66 us (1%)
    pallas_call x1, Pallas kernels, shards(): pl.pallas_call(functools.partial(kernel, modes, slabs, group), out_shape=...  53.9 us
    pallas_call x1, Pallas kernels, shards(): pl.pallas_call(functools.partial(finish_kernel, pieces), out_shape=[jax.S...  3.54 us

profile of v2, /device:TPU:0, one launch (start us, length us, event | category | flops | bytes accessed | tf_op | source)
XLA Modules:
  0.0 58.1 jit_solution(5186635660838631374)
XLA Ops:
  0.6 0.0 copy-start
  0.6 53.9 %gather_mix.1 = (f32[64,16384]{1,0:T(8,128)S(1)}, f32[64,16384]{1,0:T(8,128)S(1)}) custom-call(f32[64,16384]{1,0:T(8,128)} %field.1, f32[64,16384]{1,0:T(8,128)} %right.1, f32[2,16384]{1,0:T(2,128)} %coefficient.1, bf16[2,7,256,256]{3,2,1,0:T(8,128)(2,1)} %blocks.1, s32[7,64]{1,0:T(8,128)} %bitcast.6, bf16[16,16,48]{2,1,0:T(8,128)(2,1)} %bitcast.5, ...), custom_call_target="tpu_custom_call" | custom-call | tf_op jit(solution)/shard_map/gather_mix/pallas_call | solution.py:283
  54.6 0.0 copy-done
  54.6 3.5 %finish.1 = (f32[64,16384]{1,0:T(8,128)}, f32[64,16384]{1,0:T(8,128)}) custom-call(f32[64,16384]{1,0:T(8,128)S(1)} %get-tuple-element.4.field, f32[64,16384]{1,0:T(8,128)S(1)} %get-tuple-element.5.found, f32[1,16384]{1,0:T(1,128)S(1)} %bitcast.4), custom_call_target="tpu_custom_call" | custom-call | tf_op jit(solution)/shard_map/finish/pallas_call | solution.py:304
Async XLA Ops:
  0.6 53.9 %copy-start = (f32[16384]{0:T(1024)S(1)}, f32[16384]{0:T(1024)}, u32[]{:S(2)}) copy-start(f32[16384]{0:T(1024)} %param.11) | copy-start | bytes 196612

commit v3 on v2

--- a/solution.py
+++ b/solution.py
@@ -182,7 +182,7 @@
     for i in range(part):
         spread_out = lax.dot_general(
             chaos_values[i], repeat, (((0,), (0,)), ((), ())), preferred_element_type=jnp.float32)
-        placed = (spread_out * hits[...]).astype(jnp.bfloat16)
+        placed = (spread_out * hits[0:links, :]).astype(jnp.bfloat16)
         mine = jnp.logical_and(owned, lax.rem(row_of, part) == i).astype(jnp.float32).astype(jnp.bfloat16)
         built = built + jnp.dot(mine, placed, preferred_element_type=jnp.float32)
     matrix[...] = built.astype(jnp.bfloat16)
@@ -231,6 +231,291 @@
         for j, peer in enumerate(peers):
             send(me, g, peer, far_send.at[j, g]).wait_send()
             send(peer, g, sibling, forward_send.at[j, g]).wait_send()
+
+    @pl.when(has_left)
+    def _():
+        to_left.wait_send()
+
+    @pl.when(has_right)
+    def _():
+        to_right.wait_send()
+
+
+def packed_kernel(
+    modes, slabs, group, packed,
+    field, right, coefficient, blocks, couplings, chaos_values, chaos_index,
+    fbuf, rbuf,
+    low, weights, coef, gathered, outgoing, arrived, matrix, hits, picks,
+    field_sem, right_sem, weight_sem, coef_sem,
+    halo_send, halo_recv, near_send, near_recv, far_send, far_recv, forward_send, forward_recv,
+):
+    rows, width = field.shape
+    size = blocks.shape[-1]
+    count = width // size
+    groups = count // group
+    span = group * size
+    taps = 2 * REACH + 1
+    pairs = modes // 2
+    me = lax.axis_index("mode")
+    slab = lax.axis_index("mesh")
+    sibling = me + 1 - 2 * lax.rem(me, 2)
+    peer = lax.rem(me + 2, modes)
+    peers = [peer]
+    core = lax.rem(me, 2)
+    here = me // 2
+    there = peer // 2
+    share = group // 2
+    has_left = slab > 0
+    has_right = slab < slabs - 1
+
+    def columns(g):
+        return pl.ds(pl.multiple_of(g * span, span), span)
+
+    def field_copy(g):
+        return pltpu.make_async_copy(field.at[:, columns(g)], fbuf.at[:, columns(g)], field_sem.at[g])
+
+    def right_copy(g):
+        return pltpu.make_async_copy(right.at[:, columns(g)], rbuf.at[:, columns(g)], right_sem.at[g])
+
+    def weight_copy(k):
+        return pltpu.make_async_copy(blocks.at[k], weights.at[k], weight_sem.at[k])
+
+    field_copy(0).start()
+    field_copy(groups - 1).start()
+    weight_copy(1).start()
+    coef_copy = pltpu.make_async_copy(coefficient, coef, coef_sem)
+    coef_copy.start()
+
+    @pl.loop(1, groups - 1)
+    def _(g):
+        field_copy(g).start()
+
+    weight_copy(0).start()
+
+    @pl.loop(0, groups)
+    def _(g):
+        right_copy(g).start()
+
+    barrier = pltpu.get_barrier_semaphore()
+    for other in [sibling] + peers:
+        pl.semaphore_signal(barrier, inc=1, device_id={"mode": other}, device_id_type=MESH)
+
+    @pl.when(has_left)
+    def _():
+        pl.semaphore_signal(barrier, inc=1, device_id={"mesh": slab - 1}, device_id_type=MESH)
+
+    @pl.when(has_right)
+    def _():
+        pl.semaphore_signal(barrier, inc=1, device_id={"mesh": slab + 1}, device_id_type=MESH)
+
+    def lower(g):
+        for b in range(group):
+            at = g * group + b
+            cols = pl.ds(pl.multiple_of(at * size, size), size)
+            low[REACH + at] = fbuf[:, cols].astype(jnp.bfloat16)
+
+    part, _, links = chaos_values.shape
+    total_rows = modes * rows
+    per_row = links * part // total_rows
+    column_of = lax.broadcasted_iota(jnp.int32, (1, total_rows), 1) // part
+    for n in range(links):
+        hits[n:n + 1, :] = (column_of == chaos_index[1, n]).astype(jnp.float32)
+    both = 2 * rows
+    tall = packed * part
+    lanes = lax.broadcasted_iota(jnp.int32, (1, total_rows), 1)
+    pair_of_entry = lax.broadcasted_iota(jnp.int32, (links, total_rows), 0) // per_row * part // both
+    earlier = jnp.logical_and(
+        lax.broadcasted_iota(jnp.int32, (total_rows, total_rows), 0) // part
+        < lax.broadcasted_iota(jnp.int32, (total_rows, total_rows), 1) // part,
+        jnp.logical_and(
+            lax.broadcasted_iota(jnp.int32, (total_rows, total_rows), 0) // both
+            == lax.broadcasted_iota(jnp.int32, (total_rows, total_rows), 1) // both,
+            lax.rem(lax.broadcasted_iota(jnp.int32, (total_rows, total_rows), 0), part) == 0))
+    earlier = earlier.astype(jnp.float32).astype(jnp.bfloat16)
+
+    def picked(source, target):
+        wanted = jnp.max(jnp.where(pair_of_entry == target, hits[0:links, :], 0.0), axis=0, keepdims=True)
+        wanted = jnp.where(lanes // both == source, wanted, 0.0)
+        before = jnp.dot(
+            jnp.broadcast_to(wanted, (8, total_rows)).astype(jnp.bfloat16), earlier,
+            preferred_element_type=jnp.float32)[0:1]
+        place = before * part + lax.rem(lanes, part).astype(jnp.float32)
+        row = lax.broadcasted_iota(jnp.int32, (tall, total_rows), 0).astype(jnp.float32)
+        return jnp.where(jnp.logical_and(row == place, wanted > 0.0), 1.0, 0.0).astype(jnp.bfloat16)
+
+    picks[...] = picked(here, there)
+
+    field_copy(0).wait()
+    lower(0)
+    field_copy(groups - 1).wait()
+    lower(groups - 1)
+
+    pl.semaphore_wait(barrier, pairs + jnp.minimum(slab, 1) + jnp.minimum(slabs - 1 - slab, 1))
+
+    to_left = pltpu.make_async_remote_copy(
+        src_ref=low.at[pl.ds(REACH, REACH)], dst_ref=low.at[pl.ds(REACH + count, REACH)],
+        send_sem=halo_send.at[0], recv_sem=halo_recv.at[0],
+        device_id={"mesh": slab - 1}, device_id_type=MESH)
+    to_right = pltpu.make_async_remote_copy(
+        src_ref=low.at[pl.ds(count, REACH)], dst_ref=low.at[pl.ds(0, REACH)],
+        send_sem=halo_send.at[1], recv_sem=halo_recv.at[1],
+        device_id={"mesh": slab + 1}, device_id_type=MESH)
+
+    @pl.when(has_left)
+    def _():
+        to_left.start()
+
+    @pl.when(has_right)
+    def _():
+        to_right.start()
+
+    @pl.when(jnp.logical_not(has_left))
+    def _():
+        low[pl.ds(0, REACH)] = jnp.zeros((REACH, rows, size), jnp.bfloat16)
+
+    @pl.when(jnp.logical_not(has_right))
+    def _():
+        low[pl.ds(REACH + count, REACH)] = jnp.zeros((REACH, rows, size), jnp.bfloat16)
+
+    field_copy(1).wait()
+    lower(1)
+    weight_copy(1).wait()
+    coef_copy.wait()
+
+    def stencil(g, k):
+        tall = []
+        for b in range(group):
+            at = g * group + b
+            wide = []
+            for c in range(taps):
+                keep = jnp.full((rows, size), couplings[c, at].astype(jnp.float32)).astype(jnp.bfloat16)
+                wide.append(low[at + c] * keep)
+            tall.append(jnp.concatenate(wide, axis=1))
+        stacked = jnp.concatenate(tall, axis=0)
+        return jnp.dot(stacked, weights[k].reshape(taps * size, size), preferred_element_type=jnp.float32)
+
+    def near(g):
+        held = gathered.at[core, pl.ds(g * group, group)]
+        return pltpu.make_async_remote_copy(
+            src_ref=held, dst_ref=held, send_sem=near_send.at[g], recv_sem=near_recv.at[g],
+            device_id={"mode": sibling}, device_id_type=MESH)
+
+    def far(g):
+        return pltpu.make_async_remote_copy(
+            src_ref=outgoing.at[pl.ds(g * share, share)],
+            dst_ref=arrived.at[pl.ds(g * group + core * share, share)],
+            send_sem=far_send.at[g], recv_sem=far_recv.at[g],
+            device_id={"mode": peer}, device_id_type=MESH)
+
+    def relay(g):
+        held = arrived.at[pl.ds(g * group + core * share, share)]
+        return pltpu.make_async_remote_copy(
+            src_ref=held, dst_ref=held, send_sem=forward_send.at[g], recv_sem=forward_recv.at[g],
+            device_id={"mode": sibling}, device_id_type=MESH)
+
+    def pack(g):
+        near(g).wait_recv()
+        chosen = picks[:, pl.ds(pl.multiple_of(here * both, both), both)]
+        for b in range(share):
+            at = g * group + core * share + b
+            outgoing[g * share + b] = jnp.dot(
+                chosen, gathered[:, at].reshape(both, size),
+                preferred_element_type=jnp.float32).astype(jnp.bfloat16)
+        far(g).start()
+
+    def turn(t):
+        return lax.rem(t + 1, groups)
+
+    @pl.loop(0, groups)
+    def _(t):
+        g = turn(t)
+
+        @pl.when(t + 2 <= groups - 2)
+        def _():
+            field_copy(t + 2).wait()
+            lower(t + 2)
+
+        @pl.when(jnp.logical_and(t == groups - 2, has_right))
+        def _():
+            to_left.wait_recv()
+
+        @pl.when(jnp.logical_and(t == groups - 1, has_left))
+        def _():
+            to_right.wait_recv()
+
+        sums = stencil(g, 1)
+        for b in range(group):
+            at = g * group + b
+            cols = pl.ds(pl.multiple_of(at * size, size), size)
+            scaled = sums[b * rows:(b + 1) * rows] * coef[1:2, cols]
+            gathered[core, at] = scaled.astype(jnp.bfloat16)
+        near(g).start()
+
+        @pl.when(t > 0)
+        def _():
+            pack(turn(t - 1))
+
+    pack(turn(groups - 1))
+
+    lane_of = lax.broadcasted_iota(jnp.int32, (part, total_rows), 1)
+    step_of = lax.broadcasted_iota(jnp.int32, (part, total_rows), 0)
+    repeat = (lax.rem(lane_of, part) == step_of).astype(jnp.float32).astype(jnp.bfloat16)
+    row_of = lax.broadcasted_iota(jnp.int32, (rows, links), 0)
+    owner_of = lax.broadcasted_iota(jnp.int32, (rows, links), 1) // per_row
+    owned = owner_of == row_of // part + me * (rows // part)
+    built = jnp.zeros((rows, total_rows), jnp.float32)
+    for i in range(part):
+        spread_out = lax.dot_general(
+            chaos_values[i], repeat, (((0,), (0,)), ((), ())), preferred_element_type=jnp.float32)
+        placed = (spread_out * hits[0:links, :]).astype(jnp.bfloat16)
+        mine = jnp.logical_and(owned, lax.rem(row_of, part) == i).astype(jnp.float32).astype(jnp.bfloat16)
+        built = built + jnp.dot(mine, placed, preferred_element_type=jnp.float32)
+    built = built.astype(jnp.bfloat16)
+    matrix[:, both:both + tall] = lax.dot_general(
+        built, picked(there, here), (((1,), (1,)), ((), ())),
+        preferred_element_type=jnp.float32).astype(jnp.bfloat16)
+    hits[0:rows, :] = built.astype(jnp.float32)
+    matrix[:, 0:both] = hits[0:rows, pl.ds(pl.multiple_of(here * both, both), both)].astype(jnp.bfloat16)
+
+    weight_copy(0).wait()
+
+    @pl.loop(0, groups)
+    def _(t):
+        g = turn(t)
+        right_copy(g).wait()
+        sums = stencil(g, 0)
+        for b in range(group):
+            at = g * group + b
+            cols = pl.ds(pl.multiple_of(at * size, size), size)
+            rbuf[:, cols] = rbuf[:, cols] - sums[b * rows:(b + 1) * rows] * coef[0:1, cols]
+
+    def mix(g):
+        relay(g).wait_recv()
+        for b in range(group):
+            at = g * group + b
+            cols = pl.ds(pl.multiple_of(at * size, size), size)
+            stacked = jnp.concatenate([gathered[:, at].reshape(both, size), arrived[at]], axis=0)
+            mixed = jnp.dot(matrix[...], stacked, preferred_element_type=jnp.float32)
+            rbuf[:, cols] = rbuf[:, cols] - mixed
+
+    def forward(g):
+        far(g).wait_recv()
+        relay(g).start()
+
+    forward(turn(0))
+
+    @pl.loop(1, groups)
+    def _(t):
+        forward(turn(t))
+        mix(turn(t - 1))
+
+    mix(turn(groups - 1))
+
+    @pl.loop(0, groups)
+    def _(g):
+        near(g).wait_send()
+        far(g).wait_send()
+        relay(g).wait_send()
 
     @pl.when(has_left)
     def _():
@@ -265,6 +550,17 @@
     def _(i):
         found_copy(i).wait()
         stage_copy(i).wait()
+
+
+def choose_kernel(held, fewest, chaos_index, choice):
+    entries = chaos_index.shape[1]
+    seen = jnp.int32(0)
+    for n in range(entries):
+        column = chaos_index[1, n]
+        crosses = column // held != n * 2 * held // entries // held
+        seen = seen | jnp.where(crosses, jnp.int32(1) << column, 0)
+    counts = [sum((seen >> (side * held + i)) & 1 for i in range(held)) for side in range(2)]
+    choice[0, 0] = jnp.maximum(jnp.maximum(counts[0], counts[1]) - fewest, 0)
 
 
 def shards(modes, slabs, field, right_side, coefficient, precond, blocks, couplings, chaos_values, chaos_index):
@@ -280,36 +576,81 @@
     spare = 67043328 - 2 * rows * width * 4 - 96 * 1024
     scalars = pl.BlockSpec(memory_space=pltpu.SMEM)
     dma = pltpu.SemaphoreType.DMA
-    kept, found = pl.pallas_call(
-        functools.partial(kernel, modes, slabs, group),
-        out_shape=[pltpu.VMEM((rows, width), jnp.float32)] * 2,
-        in_specs=[anywhere, anywhere, anywhere, anywhere, scalars, pl.BlockSpec(memory_space=pltpu.VMEM), scalars],
-        out_specs=[inside] * 2,
-        scratch_shapes=[
-            pltpu.VMEM((count + 2 * REACH, rows, size), jnp.bfloat16),
-            pltpu.VMEM(blocks.shape, jnp.bfloat16),
-            pltpu.VMEM(coefficient.shape, jnp.float32),
-            pltpu.VMEM((modes, count, rows, size), jnp.bfloat16),
-            pltpu.VMEM((rows, modes * rows), jnp.bfloat16),
-            pltpu.VMEM((chaos_values.shape[0], modes * rows), jnp.float32),
-            dma((groups,)), dma((groups,)), dma((2,)), dma,
-            dma((2,)), dma((2,)), dma((groups,)), dma((others, groups)), dma((others, groups)),
-            dma((modes, groups)),
-        ],
-        compiler_params=pltpu.CompilerParams(
-            collective_id=0, has_side_effects=True, vmem_limit_bytes=spare),
-        name="gather_mix",
-    )(field, right_side, coefficient, blocks, couplings.T, chaos_values.transpose(1, 2, 0), chaos_index.T)
-    pieces = 16
-    return pl.pallas_call(
-        functools.partial(finish_kernel, pieces),
-        out_shape=[jax.ShapeDtypeStruct((rows, width), jnp.float32)] * 2,
-        in_specs=[inside] * 3,
-        out_specs=[anywhere] * 2,
-        scratch_shapes=[pltpu.VMEM((rows, width), jnp.float32), dma((2, pieces))],
-        compiler_params=pltpu.CompilerParams(vmem_limit_bytes=8 * 1024 * 1024),
-        name="finish",
-    )(kept, found, precond[None, :])
+    part = chaos_values.shape[1]
+    both = 2 * rows
+    entries = chaos_values.shape[0]
+    common = [
+        pltpu.VMEM((count + 2 * REACH, rows, size), jnp.bfloat16),
+        pltpu.VMEM(blocks.shape, jnp.bfloat16),
+        pltpu.VMEM(coefficient.shape, jnp.float32),
+    ]
+    waits = [dma((groups,)), dma((groups,)), dma((2,)), dma, dma((2,)), dma((2,))]
+    hits = pltpu.VMEM((max(entries, rows), modes * rows), jnp.float32)
+
+    def whole(*operands):
+        return run(
+            functools.partial(kernel, modes, slabs, group), 0,
+            common + [
+                pltpu.VMEM((modes, count, rows, size), jnp.bfloat16),
+                pltpu.VMEM((rows, modes * rows), jnp.bfloat16),
+                hits,
+            ] + waits + [dma((groups,)), dma((others, groups)), dma((others, groups)), dma((modes, groups))],
+            operands)
+
+    def reduced(packed, *operands):
+        tall = packed * part
+        return run(
+            functools.partial(packed_kernel, modes, slabs, group, packed), packed,
+            common + [
+                pltpu.VMEM((2, count, rows, size), jnp.bfloat16),
+                pltpu.VMEM((count // 2, tall, size), jnp.bfloat16),
+                pltpu.VMEM((count, tall, size), jnp.bfloat16),
+                pltpu.VMEM((rows, both + tall), jnp.bfloat16),
+                hits,
+                pltpu.VMEM((tall, modes * rows), jnp.bfloat16),
+            ] + waits + [dma((groups,))] * 6,
+            operands)
+
+    def run(body, ident, scratch, operands):
+        kept, found = pl.pallas_call(
+            body,
+            out_shape=[pltpu.VMEM((rows, width), jnp.float32)] * 2,
+            in_specs=[anywhere, anywhere, anywhere, anywhere, scalars, inside, scalars],
+            out_specs=[inside] * 2,
+            scratch_shapes=scratch,
+            compiler_params=pltpu.CompilerParams(
+                collective_id=ident, has_side_effects=True, vmem_limit_bytes=spare),
+            name="gather_mix",
+        )(*operands[1:])
+        pieces = 16
+        return tuple(pl.pallas_call(
+            functools.partial(finish_kernel, pieces),
+            out_shape=[jax.ShapeDtypeStruct((rows, width), jnp.float32)] * 2,
+            in_specs=[inside] * 3,
+            out_specs=[anywhere] * 2,
+            scratch_shapes=[pltpu.VMEM((rows, width), jnp.float32), dma((2, pieces))],
+            compiler_params=pltpu.CompilerParams(vmem_limit_bytes=8 * 1024 * 1024),
+            name="finish",
+        )(kept, found, operands[0]))
+
+    operands = (
+        precond[None, :], field, right_side, coefficient, blocks, couplings.T,
+        chaos_values.transpose(1, 2, 0), chaos_index.T)
+    if modes != 4 or both % part:
+        return whole(*operands)
+    held = both // part
+    fewest = held // 2 + 1
+    choice = pl.pallas_call(
+        functools.partial(choose_kernel, held, fewest),
+        out_shape=jax.ShapeDtypeStruct((1, 1), jnp.int32),
+        in_specs=[scalars],
+        out_specs=scalars,
+        name="choose",
+    )(operands[-1])
+    return lax.switch(
+        choice[0, 0],
+        [functools.partial(reduced, packed) for packed in range(fewest, held + 1)],
+        *operands)
 
 
 def solution(mesh):

time: 58.4 us -> 50.8 us (0.87)
  Pallas kernels: 57.5 us -> 49.2 us
  between operations: 0.66 us -> 1.29 us
    pallas_call x2 -> x3, Pallas kernels: 57.5 us -> 49.2 us  [the longest x1 44.2 us: run(): pl.pallas_call(body, out_shape=[pltpu.VMEM((rows, width), jnp.float32)] *...]
where the time goes in v3:
time: 50.8 us; the launch traced here: 50.6 us
  Pallas kernels  49.2 us (97%)
  between operations  1.29 us (3%)
    pallas_call x1, Pallas kernels, run(): pl.pallas_call(body, out_shape=[pltpu.VMEM((rows, width), jnp.float32)] *...  44.2 us
    pallas_call x1, Pallas kernels, run(): pl.pallas_call(functools.partial(finish_kernel, pieces), out_shape=[jax.S...  3.54 us
    pallas_call x1, Pallas kernels, shards(): pl.pallas_call(functools.partial(choose_kernel, held, fewest), out_shape=...  1.49 us

profile of v3, /device:TPU:0, one launch (start us, length us, event | category | flops | bytes accessed | tf_op | source)
XLA Modules:
  0.0 50.6 jit_solution(8707345591128987351)
XLA Ops:
  0.6 1.5 %choose.1 = s32[1,1]{1,0:T(1,128)} custom-call(s32[2,48]{1,0:T(2,128)} %bitcast.20), custom_call_target="tpu_custom_call" | custom-call | tf_op jit(solution)/shard_map/choose/pallas_call | solution.py:643
  2.8 47.8 %conditional.1 = ((f32[64,16384]{1,0:T(8,128)}, f32[64,16384]{1,0:T(8,128)})) conditional(s32[]{:T(128)} %bitcast.5, (f32[64,16384]{1,0:T(8,128)}, f32[64,16384]{1,0:T(8,128)}, f32[2,16384]{1,0:T(2,128)}, bf16[2,7,256,256]{3,2,1,0:T(8,128)(2,1)}, s32[7,64]{1,0:T(8,128)}, /*index=5*/bf16[16,16,48]{2,1,0:T(8,128)(2,1)}, ...), branch_computations={%region_0.0_spmd, %region_1.0_spmd, %region_2.0_spmd, %region_3.0_... | conditional | bytes 262180 | solution.py:650
  2.8 0.0 copy-start.1
  2.8 44.2 %gather_mix.5 = (f32[64,16384]{1,0:T(8,128)S(1)}, f32[64,16384]{1,0:T(8,128)S(1)}) custom-call(f32[64,16384]{1,0:T(8,128)} %get-tuple-element.137.field, f32[64,16384]{1,0:T(8,128)} %get-tuple-element.141.right, f32[2,16384]{1,0:T(2,128)} %get-tuple-element.145.coefficient, bf16[2,7,256,256]{3,2,1,0:T(8,128)(2,1)} %get-tuple-element.149.blocks, ...), custom_call_target="tpu_custom_call" | custom-call | tf_op jit(solution)/shard_map/cond/branch_1_fun/gather_mix/pallas_call | solution.py:615
  47.0 0.0 copy-done.1
  47.0 3.5 %finish.5 = (f32[64,16384]{1,0:T(8,128)}, f32[64,16384]{1,0:T(8,128)}) custom-call(f32[64,16384]{1,0:T(8,128)S(1)} %get-tuple-element.81.field, f32[64,16384]{1,0:T(8,128)S(1)} %get-tuple-element.82.found, f32[1,16384]{1,0:T(1,128)S(1)} %bitcast.13), custom_call_target="tpu_custom_call" | custom-call | tf_op jit(solution)/shard_map/cond/branch_1_fun/finish/pallas_call | solution.py:626
Async XLA Ops:
  2.8 44.2 %copy-start.1 = (f32[16384]{0:T(1024)S(1)}, f32[16384]{0:T(1024)}, u32[]{:S(2)}) copy-start(f32[16384]{0:T(1024)} %get-tuple-element.157) | copy-start | bytes 196612 | tf_op jit(solution)/shard_map/cond

commit v4 on v3

--- a/solution.py
+++ b/solution.py
@@ -423,6 +423,14 @@
                 preferred_element_type=jnp.float32).astype(jnp.bfloat16)
         far(g).start()
 
+    def settle(g):
+        right_copy(g).wait()
+        sums = stencil(g, 0)
+        for b in range(group):
+            at = g * group + b
+            cols = pl.ds(pl.multiple_of(at * size, size), size)
+            rbuf[:, cols] = rbuf[:, cols] - sums[b * rows:(b + 1) * rows] * coef[0:1, cols]
+
     def turn(t):
         return lax.rem(t + 1, groups)
 
@@ -451,11 +459,17 @@
             gathered[core, at] = scaled.astype(jnp.bfloat16)
         near(g).start()
 
+        @pl.when(t == 1)
+        def _():
+            weight_copy(0).wait()
+
         @pl.when(t > 0)
         def _():
             pack(turn(t - 1))
+            settle(turn(t - 1))
 
     pack(turn(groups - 1))
+    settle(turn(groups - 1))
 
     lane_of = lax.broadcasted_iota(jnp.int32, (part, total_rows), 1)
     step_of = lax.broadcasted_iota(jnp.int32, (part, total_rows), 0)
@@ -476,18 +490,6 @@
         preferred_element_type=jnp.float32).astype(jnp.bfloat16)
     hits[0:rows, :] = built.astype(jnp.float32)
     matrix[:, 0:both] = hits[0:rows, pl.ds(pl.multiple_of(here * both, both), both)].astype(jnp.bfloat16)
-
-    weight_copy(0).wait()
-
-    @pl.loop(0, groups)
-    def _(t):
-        g = turn(t)
-        right_copy(g).wait()
-        sums = stencil(g, 0)
-        for b in range(group):
-            at = g * group + b
-            cols = pl.ds(pl.multiple_of(at * size, size), size)
-            rbuf[:, cols] = rbuf[:, cols] - sums[b * rows:(b + 1) * rows] * coef[0:1, cols]
 
     def mix(g):
         relay(g).wait_recv()

time: 50.8 us -> 56.6 us (1.11)
  Pallas kernels: 49.2 us -> 55.1 us
    pallas_call x1, Pallas kernels: 44.2 us -> 50 us  [run(): pl.pallas_call(body, out_shape=[pltpu.VMEM((rows, width), jnp.float32)] *...]
where the time goes in v4:
time: 56.6 us; the launch traced here: 56.4 us
  Pallas kernels  55.1 us (97%)
  between operations  1.29 us (2%)
    pallas_call x1, Pallas kernels, run(): pl.pallas_call(body, out_shape=[pltpu.VMEM((rows, width), jnp.float32)] *...  50 us
    pallas_call x1, Pallas kernels, run(): pl.pallas_call(functools.partial(finish_kernel, pieces), out_shape=[jax.S...  3.54 us
    pallas_call x1, Pallas kernels, shards(): pl.pallas_call(functools.partial(choose_kernel, held, fewest), out_shape=...  1.49 us

profile of v4, /device:TPU:0, one launch (start us, length us, event | category | flops | bytes accessed | tf_op | source)
XLA Modules:
  0.0 56.4 jit_solution(11005173283724380316)
XLA Ops:
  0.6 1.5 %choose.1 = s32[1,1]{1,0:T(1,128)} custom-call(s32[2,48]{1,0:T(2,128)} %bitcast.20), custom_call_target="tpu_custom_call" | custom-call | tf_op jit(solution)/shard_map/choose/pallas_call | solution.py:645
  2.8 53.6 %conditional.1 = ((f32[64,16384]{1,0:T(8,128)}, f32[64,16384]{1,0:T(8,128)})) conditional(s32[]{:T(128)} %bitcast.5, (f32[64,16384]{1,0:T(8,128)}, f32[64,16384]{1,0:T(8,128)}, f32[2,16384]{1,0:T(2,128)}, bf16[2,7,256,256]{3,2,1,0:T(8,128)(2,1)}, s32[7,64]{1,0:T(8,128)}, /*index=5*/bf16[16,16,48]{2,1,0:T(8,128)(2,1)}, ...), branch_computations={%region_0.0_spmd, %region_1.0_spmd, %region_2.0_spmd, %region_3.0_... | conditional | bytes 262180 | solution.py:652
  2.8 0.0 copy-start.2
  2.8 50.0 %gather_mix.6 = (f32[64,16384]{1,0:T(8,128)S(1)}, f32[64,16384]{1,0:T(8,128)S(1)}) custom-call(f32[64,16384]{1,0:T(8,128)} %get-tuple-element.138.field, f32[64,16384]{1,0:T(8,128)} %get-tuple-element.142.right, f32[2,16384]{1,0:T(2,128)} %get-tuple-element.146.coefficient, bf16[2,7,256,256]{3,2,1,0:T(8,128)(2,1)} %get-tuple-element.150.blocks, ...), custom_call_target="tpu_custom_call" | custom-call | tf_op jit(solution)/shard_map/cond/branch_2_fun/gather_mix/pallas_call | solution.py:617
  52.8 0.0 copy-done.2
  52.8 3.5 %finish.6 = (f32[64,16384]{1,0:T(8,128)}, f32[64,16384]{1,0:T(8,128)}) custom-call(f32[64,16384]{1,0:T(8,128)S(1)} %get-tuple-element.91.field, f32[64,16384]{1,0:T(8,128)S(1)} %get-tuple-element.92.found, f32[1,16384]{1,0:T(1,128)S(1)} %bitcast.14), custom_call_target="tpu_custom_call" | custom-call | tf_op jit(solution)/shard_map/cond/branch_2_fun/finish/pallas_call | solution.py:628
Async XLA Ops:
  2.8 50.0 %copy-start.2 = (f32[16384]{0:T(1024)S(1)}, f32[16384]{0:T(1024)}, u32[]{:S(2)}) copy-start(f32[16384]{0:T(1024)} %get-tuple-element.158) | copy-start | bytes 196612 | tf_op jit(solution)/shard_map/cond
